TPU v7x, 32 devices: a whole 2x2x4 slice. The times are simulated.
32 devices in a mesh: cell: 2 (over y), gene: 16 (over z, x, core).
Axes of the slice: x: 2, y: 2, z: 4, core: 2. Of those that a mesh axis runs over, the one named last changes fastest.
Arguments:
- blocks: bfloat16 [1536, 256, 256], P(('cell', 'gene')), may hold values from 0 to 255, as said below
- block_rows: int32 [1536], P(('cell', 'gene')), may hold values from 0 to 15, as said below
- block_cols: int32 [1536], P(('cell', 'gene')), may hold values from 0 to 3, as said below
- block_count: int32 [32], P(('cell', 'gene')), may hold values from 2 to 48, as said below
- cell_factor: float32 [8192, 128], P(('cell', 'gene')), as said below
- gene_factor: float32 [16384, 128], P('gene'), as said below
Outputs:
- cell_new: float32 [8192, 128], P(('cell', 'gene'))
- gene_new: float32 [16384, 128], P('gene')
Inputs may be any that keep to these rules, and one draw needn't show every extreme that they name: `blocks`: counts are whole numbers. `block_rows`: within one device the live slots and the padding slots name distinct block positions. `block_cols`: within one device the live slots and the padding slots name distinct block positions. `block_count`: some device has all 48 slots live. `cell_factor`: positive entries. `gene_factor`: positive entries.
All inputs are finite; a program needn't handle non-finite values.
Results may differ from a plain program's by a relative error of at most 0.00084.
Values may be sent and summed in bfloat16 or wider, within the bound.
A program may use at most 64 MiB of HBM per device.

v0:
```python
import jax
import jax.numpy as jnp
from jax import lax
from jax.sharding import PartitionSpec as P


def block_ratio(blocks, row_tiles, col_tiles, live):
    model = jnp.einsum("nir,njr->nij", row_tiles, col_tiles, preferred_element_type=jnp.float32)
    return (blocks.astype(jnp.float32) / model * live[:, None, None]).astype(jnp.bfloat16)


def on_device(blocks, block_rows, block_cols, block_count, cell_factor, gene_factor):
    slots = blocks.shape[0]
    width = blocks.shape[1]
    rank = cell_factor.shape[1]
    gene_len = gene_factor.shape[0]
    live = (jnp.arange(slots, dtype=jnp.int32) < block_count[0]).astype(jnp.float32)
    gene_bf = gene_factor.astype(jnp.bfloat16)
    gene_tiles = gene_bf.reshape(-1, width, rank)[block_cols]
    gene_totals = lax.psum(jnp.sum(gene_factor, 0), "gene")
    cell_full = lax.all_gather(cell_factor, "gene", axis=0, tiled=True)
    cell_bf = cell_full.astype(jnp.bfloat16)
    row_count = cell_bf.shape[0] // width
    row_pick = (block_rows[None, :] == jnp.arange(row_count, dtype=jnp.int32)[:, None]).astype(
        jnp.float32
    )
    col_pick = (
        block_cols[None, :] == jnp.arange(gene_len // width, dtype=jnp.int32)[:, None]
    ).astype(jnp.float32)
    row_tiles = cell_bf.reshape(row_count, width, rank)[block_rows]
    ratio = block_ratio(blocks, row_tiles, gene_tiles, live)
    terms = jnp.einsum("nij,njr->nir", ratio, gene_tiles, preferred_element_type=jnp.float32)
    numer = jnp.einsum("bn,nir->bir", row_pick, terms, precision=lax.Precision.HIGHEST).reshape(
        -1, rank
    )
    whole = lax.psum(numer, "gene")
    group_new = cell_full * whole / gene_totals
    new_bf = group_new.astype(jnp.bfloat16)
    cell_sums = lax.psum(jnp.sum(group_new, 0), "cell")
    own_rows = cell_factor.shape[0]
    cell_new = lax.dynamic_slice_in_dim(group_new, lax.axis_index("gene") * own_rows, own_rows, 0)
    new_tiles = new_bf.reshape(row_count, width, rank)[block_rows]
    ratio_next = block_ratio(blocks, new_tiles, gene_tiles, live)
    terms_next = jnp.einsum(
        "nij,nir->njr", ratio_next, new_tiles, preferred_element_type=jnp.float32
    )
    numer_gene = jnp.einsum(
        "bn,njr->bjr", col_pick, terms_next, precision=lax.Precision.HIGHEST
    ).reshape(-1, rank)
    total = lax.psum(numer_gene, "cell")
    gene_new = gene_factor * total / cell_sums
    return (cell_new, gene_new)


def solution(mesh):
    placed = (
        P(("cell", "gene"), None, None),
        P(("cell", "gene")),
        P(("cell", "gene")),
        P(("cell", "gene")),
        P(("cell", "gene"), None),
        P("gene", None),
    )
    return jax.shard_map(
        on_device,
        mesh=mesh,
        in_specs=placed,
        out_specs=(P(("cell", "gene"), None), P("gene", None)),
        check_vma=False,
    )
```

profile of v0, /device:TPU:0, one launch (start us, length us, event | category | flops | bytes accessed | tf_op | source)
XLA Modules:
  0.0 241.2 jit_solution(14404089688201856968)
XLA Ops:
  7.2 0.0 all-gather.2.cloned.1.call-start
  7.2 0.7 all-gather.2.cloned.1.call-update
  7.9 0.0 all-reduce.3.cloned.1.call-start
  8.6 0.7 compare_select_fusion
  9.3 1.4 fusion.23
  10.7 0.0 copy-start.1
  10.7 2.8 %gather_fusion.1 = bf16[48,256,128]{2,1,0:T(8,128)(2,1)} fusion(bf16[4,256,128]{2,1,0:T(8,128)(2,1)S(1)} %bitcast.19, s32[1024]{0:T(1024)S(1)} %pad_clamp_fusion), kind=kCustom, calls=%fused_computation.1 | custom fusion | bytes 6291648 | tf_op jit(solution)/shard_map/gather | solution.py:19
  13.4 0.0 copy-done.1
  13.5 40.9 %all-gather.2.cloned.1.call-done = f32[4096,128]{1,0:T(8,128)} async-done(((f32[256,128]{1,0:T(8,128)}), f32[4096,128]{1,0:T(8,128)}) %all-gather.2.cloned.1.call-update) | async-done | bytes 2097168 | tf_op jit(solution)/shard_map/all_gather | solution.py:21
  54.3 1.7 convert_element_type.29
  56.0 2.7 %gather_fusion = bf16[48,256,128]{2,1,0:T(8,128)(2,1)} fusion(bf16[16,256,128]{2,1,0:T(8,128)(2,1)S(1)} %bitcast.21, s32[1024]{0:T(1024)S(1)} %pad_clamp_fusion.1), kind=kCustom, calls=%fused_computation | custom fusion | bytes 6291648 | tf_op jit(solution)/shard_map/gather | solution.py:30
  58.7 11.7 %fusion.10 = f32[48,256,128]{2,1,0:T(8,128)} fusion(bf16[48,256,128]{2,1,0:T(8,128)(2,1)} %gather_fusion.1, bf16[48,256,256]{2,1,0:T(8,128)(2,1)} %param.6, f32[48]{0:T(128)S(1)} %compare_convert_fusion, bf16[48,256,128]{2,1,0:T(8,128)(2,1)} %gather_fusion), kind=kOutput, calls=%fused_computation.14 | convolution fusion | flops 1623195648 | bytes 18874560 | tf_op jit(solution)/shard_map/nij,njr->nir/dot_general | solution.py:32
  70.4 8.4 %fusion.6 = f32[16,256,128]{2,0,1:T(8,128)S(1)} fusion(f32[48,256,128]{2,1,0:T(8,128)} %fusion.10, s32[48]{0:T(128)S(1)} %copy-done.1), kind=kOutput, calls=%fused_computation.11 | convolution fusion | flops 301990656 | bytes 8388800 | tf_op jit(solution)/shard_map/bn,nir->bir/dot_general | solution.py:33
  78.8 2.0 copy.8
  80.8 0.0 all-reduce.3.cloned.1.call-update
  80.8 0.0 all-reduce.5.cloned.1.call-start
  80.9 31.9 %psum.29 = f32[128]{0:T(128)S(1)} all-reduce(f32[128]{0:T(128)S(1)} %get-tuple-element.5), channel_id=1, replica_groups=mesh['cell'=2,'gene'=16] {'gene'}, use_global_device_ids=true, to_apply=%region_2.0 | all-reduce | flops 128 | bytes 1024 | tf_op jit(solution)/shard_map/psum | solution.py:20
  112.8 65.2 %all-reduce.3.cloned.1.call-done = f32[4096,128]{1,0:T(8,128)} async-done(((f32[4096,128]{1,0:T(8,128)}), f32[4096,128]{1,0:T(8,128)}) %all-reduce.3.cloned.1.call-update) | async-done | bytes 2097168 | tf_op jit(solution)/shard_map/psum | solution.py:36
  177.9 2.8 %fusion.22 = (f32[128]{0:T(128)S(1)}, f32[4096,128]{1,0:T(8,128)S(1)}) fusion(f32[128]{0:T(128)S(1)} %psum.29, f32[4096,128]{1,0:T(8,128)} %all-gather.2.cloned.1.call-done, f32[4096,128]{1,0:T(8,128)} %all-reduce.3.cloned.1.call-done), kind=kLoop, calls=%fused_computation.31 | loop fusion | flops 1572736 | bytes 6292480 | tf_op jit(solution)/shard_map/reduce_sum | solution.py:39
  180.7 0.1 convert_element_type.33
  180.8 2.7 %gather_fusion.2 = bf16[48,256,128]{2,1,0:T(8,128)(2,1)} fusion(bf16[16,256,128]{2,1,0:T(8,128)(2,1)S(1)} %bitcast.20, s32[1024]{0:T(1024)S(1)} %pad_clamp_fusion.1), kind=kCustom, calls=%fused_computation.2 | custom fusion | bytes 6291648 | tf_op jit(solution)/shard_map/gather | solution.py:42
  183.5 0.0 copy-start.2
  183.5 12.2 %fusion.8 = f32[48,256,128]{2,1,0:T(8,128)} fusion(bf16[48,256,128]{2,1,0:T(8,128)(2,1)} %gather_fusion.2, bf16[48,256,256]{2,1,0:T(8,128)(2,1)} %param.6, f32[48]{0:T(128)S(1)} %compare_convert_fusion, bf16[48,256,128]{2,1,0:T(8,128)(2,1)} %gather_fusion.1), kind=kOutput, calls=%fused_computation.13 | convolution fusion | flops 1623195648 | bytes 18874560 | tf_op jit(solution)/shard_map/nij,nir->njr/dot_general | solution.py:44
  195.7 0.0 copy-done.2
  195.7 0.0 copy-start
  195.7 8.2 %fusion.4 = f32[4,256,128]{2,0,1:T(4,128)S(1)} fusion(f32[48,256,128]{2,1,0:T(8,128)} %fusion.8, s32[48]{0:T(128)S(1)} %copy-done.2), kind=kOutput, calls=%fused_computation.9 | convolution fusion | flops 75497664 | bytes 6815936 | tf_op jit(solution)/shard_map/bn,njr->bjr/dot_general | solution.py:47
  203.9 0.8 copy.9
  204.7 0.0 all-reduce.5.cloned.1.call-update
  204.7 4.9 %psum.31 = f32[128]{0:T(128)S(1)} all-reduce(f32[128]{0:T(128)S(1)} %get-tuple-element.2), channel_id=1, replica_groups=mesh['cell'=2,'gene'=16] {'cell'}, use_global_device_ids=true, to_apply=%region_5.0 | all-reduce | flops 128 | bytes 1024 | tf_op jit(solution)/shard_map/psum | solution.py:39
  209.7 0.7 constant_dynamic-slice_fusion
  210.3 22.5 %all-reduce.5.cloned.1.call-done = f32[1024,128]{1,0:T(8,128)} async-done(((f32[1024,128]{1,0:T(8,128)}), f32[1024,128]{1,0:T(8,128)}) %all-reduce.5.cloned.1.call-update) | async-done | bytes 524304 | tf_op jit(solution)/shard_map/psum | solution.py:50
  232.8 0.0 copy-done
  232.8 1.9 multiply_divide_fusion.1
  (4 shorter events, 0.0 us)
Async XLA Ops:
  7.2 47.2 %all-gather.2.cloned.1.call-start = ((), (), s32[]{:S(2)}) async-start(), calls=%async_computation | async-start | bytes 2228224 | tf_op jit(solution)/shard_map/all_gather | solution.py:21
  7.9 170.0 %all-reduce.3.cloned.1.call-start = ((), (), s32[]{:S(2)}) async-start(), calls=%async_computation.1 | async-start | bytes 4194304 | tf_op jit(solution)/shard_map/psum | solution.py:36
  10.7 2.8 %copy-start.1 = (s32[48]{0:T(128)S(1)}, s32[48]{0:T(128)}, u32[]{:S(2)}) copy-start(s32[48]{0:T(128)} %param.7) | copy-start | bytes 580
  80.8 152.0 %all-reduce.5.cloned.1.call-start = ((), (), s32[]{:S(2)}) async-start(), calls=%async_computation.2 | async-start | bytes 1048576 | tf_op jit(solution)/shard_map/psum | solution.py:50
  183.5 12.2 %copy-start.2 = (s32[48]{0:T(128)S(1)}, s32[48]{0:T(128)}, u32[]{:S(2)}) copy-start(s32[48]{0:T(128)} %param.8) | copy-start | bytes 580
  195.7 37.1 %copy-start = (f32[1024,128]{1,0:T(8,128)S(1)}, f32[1024,128]{1,0:T(8,128)}, u32[]{:S(2)}) copy-start(f32[1024,128]{1,0:T(8,128)} %param.11) | copy-start | bytes 1572868
Sparse Core Ops, SparseCore 0:
  10.1 44.1 all-gather.1
  80.9 96.9 all-reduce.2
  204.9 27.9 all-reduce.4
where the time goes:
time: 242 us; the launch traced here: 241 us
  waiting for transfers between devices  129 us (53%)
  matrix products  40.5 us (17%)
  blocking collectives  36.8 us (15%)
  between operations  14.4 us (6%)
  local copies, waits for them, and re-layouts  11.6 us (5%)
  other arithmetic  8.57 us (4%)
    psum x1, waiting for transfers between devices, on_device(): whole = lax.psum(numer, 'gene')  65.2 us
    all_gather x1, waiting for transfers between devices, on_device(): cell_full = lax.all_gather(cell_factor, 'gene', axis=0, tiled=True)  40.9 us
    psum x1, blocking collectives, on_device(): gene_totals = lax.psum(jnp.sum(gene_factor, 0), 'gene')  31.9 us
    psum x1, waiting for transfers between devices, on_device(): total = lax.psum(numer_gene, 'cell')  22.5 us
    dot_general x1, matrix products, on_device(): jnp.einsum('nij,nir->njr', ratio_next, new_tiles, preferred_element_type=...  12.2 us
    dot_general x1, matrix products, on_device(): jnp.einsum('nij,njr->nir', ratio, gene_tiles, preferred_element_type=jnp....  11.7 us
    dot_general x1, matrix products, on_device(): jnp.einsum('bn,nir->bir', row_pick, terms, precision=lax.Precision.HIGHEST)  8.37 us
    dot_general x1, matrix products, on_device(): jnp.einsum('bn,njr->bjr', col_pick, terms_next, precision=lax.Precision.H...  8.16 us
  transfers between devices with their start and end apart: 3, of which 3 were waited for; matrix products, arithmetic and copies ran while one was open for 2% of the time, Pallas kernels for 0%

commit v1 on v0

--- a/solution.py
+++ b/solution.py
@@ -18,7 +18,12 @@
     gene_bf = gene_factor.astype(jnp.bfloat16)
     gene_tiles = gene_bf.reshape(-1, width, rank)[block_cols]
     gene_totals = lax.psum(jnp.sum(gene_factor, 0), "gene")
-    cell_full = lax.all_gather(cell_factor, "gene", axis=0, tiled=True)
+    ring = [cell_factor]
+    for hop in range(15):
+        ring.append(lax.ppermute(ring[-1], "gene", [(dev, (dev + 1) % 16) for dev in range(16)]))
+    cell_full = jnp.roll(
+        jnp.concatenate(ring[::-1], axis=0), (lax.axis_index("gene") + 1) * ring[0].shape[0], axis=0
+    )
     cell_bf = cell_full.astype(jnp.bfloat16)
     row_count = cell_bf.shape[0] // width
     row_pick = (block_rows[None, :] == jnp.arange(row_count, dtype=jnp.int32)[:, None]).astype(

time: 242 us -> 302 us (1.25)
  waiting for transfers between devices: 129 us -> 190 us
    ppermute x0 -> x15, waiting for transfers between devices: none -> 101 us  [on_device(): lax.ppermute(ring[-1], 'gene', [(dev, (dev + 1) % 16) for dev in range(16)])]
    all_gather x1 -> x0, waiting for transfers between devices: 40.9 us -> none  [on_device(): cell_full = lax.all_gather(cell_factor, 'gene', axis=0, tiled=True)]
  transfers between devices with their start and end apart: 3 -> 17, of which waited for: 3 -> 17; matrix products, arithmetic and copies ran while one was open for 2% -> 2% of each run, Pallas kernels for 0% -> 0%
where the time goes in v1:
time: 302 us
  waiting for transfers between devices  190 us (63%)
  matrix products  40.5 us (13%)
  blocking collectives  35.2 us (12%)
  between operations  15 us (5%)
  local copies, waits for them, and re-layouts  14.2 us (5%)
  other arithmetic  6.89 us (2%)
    ppermute x15, waiting for transfers between devices, on_device(): lax.ppermute(ring[-1], 'gene', [(dev, (dev + 1) % 16) for dev in range(16)])  101 us
    psum x1, waiting for transfers between devices, on_device(): whole = lax.psum(numer, 'gene')  65.8 us
    psum x1, blocking collectives, on_device(): gene_totals = lax.psum(jnp.sum(gene_factor, 0), 'gene')  30.3 us
    psum x1, waiting for transfers between devices, on_device(): total = lax.psum(numer_gene, 'cell')  22.5 us
    dot_general x1, matrix products, on_device(): jnp.einsum('nij,nir->njr', ratio_next, new_tiles, preferred_element_type=...  12.2 us
    dot_general x1, matrix products, on_device(): jnp.einsum('nij,njr->nir', ratio, gene_tiles, preferred_element_type=jnp....  11.7 us
    dot_general x1, matrix products, on_device(): jnp.einsum('bn,nir->bir', row_pick, terms, precision=lax.Precision.HIGHEST)  8.37 us
    dot_general x1, matrix products, on_device(): jnp.einsum('bn,njr->bjr', col_pick, terms_next, precision=lax.Precision.H...  8.16 us
  transfers between devices with their start and end apart: 17, of which 17 were waited for; matrix products, arithmetic and copies ran while one was open for 2% of the time, Pallas kernels for 0%

profile of v1, /device:TPU:0, one launch (start us, length us, event | category | flops | bytes accessed | tf_op | source)
XLA Modules:
  0.0 302.2 jit_solution(693580109112326377)
XLA Ops:
  7.2 0.0 all-reduce.3.cloned.1.call-start
  7.2 0.5 collective-permute-start
  7.8 7.8 %collective-permute-done = f32[256,128]{1,0:T(8,128)S(1)} collective-permute-done((f32[256,128]{1,0:T(8,128)}, f32[256,128]{1,0:T(8,128)S(1)}, u32[]{:S(2)}, u32[]{:S(2)}) %collective-permute-start) | collective-permute-done | bytes 131104 | tf_op jit(solution)/shard_map/ppermute | solution.py:23
  15.6 7.1 %collective-permute-done.1 = f32[256,128]{1,0:T(8,128)S(1)} collective-permute-done((f32[256,128]{1,0:T(8,128)S(1)}, f32[256,128]{1,0:T(8,128)S(1)}, u32[]{:S(2)}, u32[]{:S(2)}) %collective-permute-start.1) | collective-permute-done | bytes 131104 | tf_op jit(solution)/shard_map/ppermute | solution.py:23
  22.7 0.0 collective-permute-start.2
  22.7 7.1 %collective-permute-done.2 = f32[256,128]{1,0:T(8,128)S(1)} collective-permute-done((f32[256,128]{1,0:T(8,128)S(1)}, f32[256,128]{1,0:T(8,128)S(1)}, u32[]{:S(2)}, u32[]{:S(2)}) %collective-permute-start.2) | collective-permute-done | bytes 131104 | tf_op jit(solution)/shard_map/ppermute | solution.py:23
  29.8 0.0 collective-permute-start.3
  29.8 7.1 %collective-permute-done.3 = f32[256,128]{1,0:T(8,128)S(1)} collective-permute-done((f32[256,128]{1,0:T(8,128)S(1)}, f32[256,128]{1,0:T(8,128)S(1)}, u32[]{:S(2)}, u32[]{:S(2)}) %collective-permute-start.3) | collective-permute-done | bytes 131104 | tf_op jit(solution)/shard_map/ppermute | solution.py:23
  36.8 7.1 %collective-permute-done.4 = f32[256,128]{1,0:T(8,128)S(1)} collective-permute-done((f32[256,128]{1,0:T(8,128)S(1)}, f32[256,128]{1,0:T(8,128)S(1)}, u32[]{:S(2)}, u32[]{:S(2)}) %collective-permute-start.4) | collective-permute-done | bytes 131104 | tf_op jit(solution)/shard_map/ppermute | solution.py:23
  43.9 0.0 collective-permute-start.5
  43.9 7.1 %collective-permute-done.5 = f32[256,128]{1,0:T(8,128)S(1)} collective-permute-done((f32[256,128]{1,0:T(8,128)S(1)}, f32[256,128]{1,0:T(8,128)S(1)}, u32[]{:S(2)}, u32[]{:S(2)}) %collective-permute-start.5) | collective-permute-done | bytes 131104 | tf_op jit(solution)/shard_map/ppermute | solution.py:23
  51.0 0.0 collective-permute-start.6
  51.0 7.1 %collective-permute-done.6 = f32[256,128]{1,0:T(8,128)S(1)} collective-permute-done((f32[256,128]{1,0:T(8,128)S(1)}, f32[256,128]{1,0:T(8,128)S(1)}, u32[]{:S(2)}, u32[]{:S(2)}) %collective-permute-start.6) | collective-permute-done | bytes 131104 | tf_op jit(solution)/shard_map/ppermute | solution.py:23
  58.1 7.1 %collective-permute-done.7 = f32[256,128]{1,0:T(8,128)S(1)} collective-permute-done((f32[256,128]{1,0:T(8,128)S(1)}, f32[256,128]{1,0:T(8,128)S(1)}, u32[]{:S(2)}, u32[]{:S(2)}) %collective-permute-start.7) | collective-permute-done | bytes 131104 | tf_op jit(solution)/shard_map/ppermute | solution.py:23
  65.2 7.1 %collective-permute-done.8 = f32[256,128]{1,0:T(8,128)S(1)} collective-permute-done((f32[256,128]{1,0:T(8,128)S(1)}, f32[256,128]{1,0:T(8,128)S(1)}, u32[]{:S(2)}, u32[]{:S(2)}) %collective-permute-start.8) | collective-permute-done | bytes 131104 | tf_op jit(solution)/shard_map/ppermute | solution.py:23
  72.3 0.0 collective-permute-start.9
  72.3 7.1 %collective-permute-done.9 = f32[256,128]{1,0:T(8,128)S(1)} collective-permute-done((f32[256,128]{1,0:T(8,128)S(1)}, f32[256,128]{1,0:T(8,128)S(1)}, u32[]{:S(2)}, u32[]{:S(2)}) %collective-permute-start.9) | collective-permute-done | bytes 131104 | tf_op jit(solution)/shard_map/ppermute | solution.py:23
  79.4 7.1 %collective-permute-done.10 = f32[256,128]{1,0:T(8,128)S(1)} collective-permute-done((f32[256,128]{1,0:T(8,128)S(1)}, f32[256,128]{1,0:T(8,128)S(1)}, u32[]{:S(2)}, u32[]{:S(2)}) %collective-permute-start.10) | collective-permute-done | bytes 131104 | tf_op jit(solution)/shard_map/ppermute | solution.py:23
  86.5 7.1 %collective-permute-done.11 = f32[256,128]{1,0:T(8,128)S(1)} collective-permute-done((f32[256,128]{1,0:T(8,128)S(1)}, f32[256,128]{1,0:T(8,128)S(1)}, u32[]{:S(2)}, u32[]{:S(2)}) %collective-permute-start.11) | collective-permute-done | bytes 131104 | tf_op jit(solution)/shard_map/ppermute | solution.py:23
  93.6 0.0 collective-permute-start.12
  93.6 1.4 fusion.23
  95.0 5.7 %collective-permute-done.12 = f32[256,128]{1,0:T(8,128)S(1)} collective-permute-done((f32[256,128]{1,0:T(8,128)S(1)}, f32[256,128]{1,0:T(8,128)S(1)}, u32[]{:S(2)}, u32[]{:S(2)}) %collective-permute-start.12) | collective-permute-done | bytes 131104 | tf_op jit(solution)/shard_map/ppermute | solution.py:23
  100.7 0.0 collective-permute-start.13
  100.7 0.7 compare_select_fusion
  102.0 5.7 %collective-permute-done.13 = f32[256,128]{1,0:T(8,128)S(1)} collective-permute-done((f32[256,128]{1,0:T(8,128)S(1)}, f32[256,128]{1,0:T(8,128)S(1)}, u32[]{:S(2)}, u32[]{:S(2)}) %collective-permute-start.13) | collective-permute-done | bytes 131104 | tf_op jit(solution)/shard_map/ppermute | solution.py:23
  107.8 2.8 gather_fusion.1
  110.6 4.3 %collective-permute-done.14 = f32[256,128]{1,0:T(8,128)S(1)} collective-permute-done((f32[256,128]{1,0:T(8,128)S(1)}, f32[256,128]{1,0:T(8,128)S(1)}, u32[]{:S(2)}, u32[]{:S(2)}) %collective-permute-start.14) | collective-permute-done | bytes 131104 | tf_op jit(solution)/shard_map/ppermute | solution.py:23
  115.5 2.0 copy-done
  117.5 0.1 dynamic-slice_convert_fusion
  117.6 2.7 gather_fusion
  120.3 11.7 %fusion.10 = f32[48,256,128]{2,1,0:T(8,128)} fusion(bf16[48,256,128]{2,1,0:T(8,128)(2,1)} %gather_fusion.1, bf16[48,256,256]{2,1,0:T(8,128)(2,1)} %param.6, f32[48]{0:T(128)S(1)} %compare_convert_fusion, bf16[48,256,128]{2,1,0:T(8,128)(2,1)} %gather_fusion), kind=kOutput, calls=%fused_computation.14 | convolution fusion | flops 1623195648 | bytes 18874560 | tf_op jit(solution)/shard_map/nij,njr->nir/dot_general | solution.py:37
  132.0 8.4 %fusion.6 = f32[16,256,128]{2,0,1:T(8,128)S(1)} fusion(f32[48,256,128]{2,1,0:T(8,128)} %fusion.10, s32[48]{0:T(128)S(1)} %copy-done.3), kind=kOutput, calls=%fused_computation.11 | convolution fusion | flops 301990656 | bytes 8388800 | tf_op jit(solution)/shard_map/bn,nir->bir/dot_general | solution.py:38
  140.4 2.0 copy.8
  142.3 0.0 all-reduce.3.cloned.1.call-update
  142.3 0.0 all-reduce.5.cloned.1.call-start
  142.4 30.3 %psum.29 = f32[128]{0:T(128)S(1)} all-reduce(f32[128]{0:T(128)S(1)} %get-tuple-element.5), channel_id=1, replica_groups=mesh['cell'=2,'gene'=16] {'gene'}, use_global_device_ids=true, to_apply=%region_2.3 | all-reduce | flops 128 | bytes 1024 | tf_op jit(solution)/shard_map/psum | solution.py:20
  172.7 65.8 %all-reduce.3.cloned.1.call-done = f32[4096,128]{1,0:T(8,128)} async-done(((f32[4096,128]{1,0:T(8,128)}), f32[4096,128]{1,0:T(8,128)}) %all-reduce.3.cloned.1.call-update) | async-done | bytes 2097168 | tf_op jit(solution)/shard_map/psum | solution.py:41
  238.5 2.8 fusion.22
  241.3 0.1 convert_element_type.33
  241.4 2.8 gather_fusion.2
  244.2 12.2 %fusion.8 = f32[48,256,128]{2,1,0:T(8,128)} fusion(bf16[48,256,128]{2,1,0:T(8,128)(2,1)} %gather_fusion.2, bf16[48,256,256]{2,1,0:T(8,128)(2,1)} %param.6, f32[48]{0:T(128)S(1)} %compare_convert_fusion, bf16[48,256,128]{2,1,0:T(8,128)(2,1)} %gather_fusion.1), kind=kOutput, calls=%fused_computation.13 | convolution fusion | flops 1623195648 | bytes 18874560 | tf_op jit(solution)/shard_map/nij,nir->njr/dot_general | solution.py:49
  256.4 8.2 %fusion.4 = f32[4,256,128]{2,0,1:T(4,128)S(1)} fusion(f32[48,256,128]{2,1,0:T(8,128)} %fusion.8, s32[48]{0:T(128)S(1)} %copy-done.4), kind=kOutput, calls=%fused_computation.9 | convolution fusion | flops 75497664 | bytes 6815936 | tf_op jit(solution)/shard_map/bn,njr->bjr/dot_general | solution.py:52
  264.6 0.8 copy.9
  265.4 0.0 all-reduce.5.cloned.1.call-update
  265.4 4.9 %psum.31 = f32[128]{0:T(128)S(1)} all-reduce(f32[128]{0:T(128)S(1)} %get-tuple-element.2), channel_id=1, replica_groups=mesh['cell'=2,'gene'=16] {'cell'}, use_global_device_ids=true, to_apply=%region_5.6 | all-reduce | flops 128 | bytes 1024 | tf_op jit(solution)/shard_map/psum | solution.py:44
  270.3 0.7 constant_dynamic-slice_fusion
  271.0 22.5 %all-reduce.5.cloned.1.call-done = f32[1024,128]{1,0:T(8,128)} async-done(((f32[1024,128]{1,0:T(8,128)}), f32[1024,128]{1,0:T(8,128)}) %all-reduce.5.cloned.1.call-update) | async-done | bytes 524304 | tf_op jit(solution)/shard_map/psum | solution.py:55
  293.5 1.9 multiply_divide_fusion.1
  (51 shorter events, 0.4 us)
Async XLA Ops:
  7.2 231.3 %all-reduce.3.cloned.1.call-start = ((), (), s32[]{:S(2)}) async-start(), calls=%async_computation | async-start | bytes 4194304 | tf_op jit(solution)/shard_map/psum | solution.py:41
  7.2 8.4 %collective-permute-start = (f32[256,128]{1,0:T(8,128)}, f32[256,128]{1,0:T(8,128)S(1)}, u32[]{:S(2)}, u32[]{:S(2)}) collective-permute-start(f32[256,128]{1,0:T(8,128)} %param.10), channel_id=1, source_target_pairs={{0,1},{1,2},{2,3},{3,4},{4,5},{5,6},{6,7},{7,8},{8,9},{9,10},{10,1... | collective-permute-start | bytes 393224 | tf_op jit(solution)/shard_map/ppermute | solution.py:23
  15.6 7.1 %collective-permute-start.1 = (f32[256,128]{1,0:T(8,128)S(1)}, f32[256,128]{1,0:T(8,128)S(1)}, u32[]{:S(2)}, u32[]{:S(2)}) collective-permute-start(f32[256,128]{1,0:T(8,128)S(1)} %collective-permute-done), channel_id=1, source_target_pairs={{0,1},{1,2},{2,3},{3,4},{4,5},{5,6},{6,7},{7,8},{8,9},{9,10},{10,1... | collective-permute-start | bytes 393224 | tf_op jit(solution)/shard_map/ppermute | solution.py:23
  22.7 7.1 %collective-permute-start.2 = (f32[256,128]{1,0:T(8,128)S(1)}, f32[256,128]{1,0:T(8,128)S(1)}, u32[]{:S(2)}, u32[]{:S(2)}) collective-permute-start(f32[256,128]{1,0:T(8,128)S(1)} %collective-permute-done.1), channel_id=1, source_target_pairs={{0,1},{1,2},{2,3},{3,4},{4,5},{5,6},{6,7},{7,8},{8,9},{9,10},{10,1... | collective-permute-start | bytes 393224 | tf_op jit(solution)/shard_map/ppermute | solution.py:23
  29.8 7.1 %collective-permute-start.3 = (f32[256,128]{1,0:T(8,128)S(1)}, f32[256,128]{1,0:T(8,128)S(1)}, u32[]{:S(2)}, u32[]{:S(2)}) collective-permute-start(f32[256,128]{1,0:T(8,128)S(1)} %collective-permute-done.2), channel_id=1, source_target_pairs={{0,1},{1,2},{2,3},{3,4},{4,5},{5,6},{6,7},{7,8},{8,9},{9,10},{10,1... | collective-permute-start | bytes 393224 | tf_op jit(solution)/shard_map/ppermute | solution.py:23
  36.8 7.1 %collective-permute-start.4 = (f32[256,128]{1,0:T(8,128)S(1)}, f32[256,128]{1,0:T(8,128)S(1)}, u32[]{:S(2)}, u32[]{:S(2)}) collective-permute-start(f32[256,128]{1,0:T(8,128)S(1)} %collective-permute-done.3), channel_id=1, source_target_pairs={{0,1},{1,2},{2,3},{3,4},{4,5},{5,6},{6,7},{7,8},{8,9},{9,10},{10,1... | collective-permute-start | bytes 393224 | tf_op jit(solution)/shard_map/ppermute | solution.py:23
  43.9 7.1 %collective-permute-start.5 = (f32[256,128]{1,0:T(8,128)S(1)}, f32[256,128]{1,0:T(8,128)S(1)}, u32[]{:S(2)}, u32[]{:S(2)}) collective-permute-start(f32[256,128]{1,0:T(8,128)S(1)} %collective-permute-done.4), channel_id=1, source_target_pairs={{0,1},{1,2},{2,3},{3,4},{4,5},{5,6},{6,7},{7,8},{8,9},{9,10},{10,1... | collective-permute-start | bytes 393224 | tf_op jit(solution)/shard_map/ppermute | solution.py:23
  51.0 7.1 %collective-permute-start.6 = (f32[256,128]{1,0:T(8,128)S(1)}, f32[256,128]{1,0:T(8,128)S(1)}, u32[]{:S(2)}, u32[]{:S(2)}) collective-permute-start(f32[256,128]{1,0:T(8,128)S(1)} %collective-permute-done.5), channel_id=1, source_target_pairs={{0,1},{1,2},{2,3},{3,4},{4,5},{5,6},{6,7},{7,8},{8,9},{9,10},{10,1... | collective-permute-start | bytes 393224 | tf_op jit(solution)/shard_map/ppermute | solution.py:23
  58.1 7.1 %collective-permute-start.7 = (f32[256,128]{1,0:T(8,128)S(1)}, f32[256,128]{1,0:T(8,128)S(1)}, u32[]{:S(2)}, u32[]{:S(2)}) collective-permute-start(f32[256,128]{1,0:T(8,128)S(1)} %collective-permute-done.6), channel_id=1, source_target_pairs={{0,1},{1,2},{2,3},{3,4},{4,5},{5,6},{6,7},{7,8},{8,9},{9,10},{10,1... | collective-permute-start | bytes 393224 | tf_op jit(solution)/shard_map/ppermute | solution.py:23
  65.2 7.1 %collective-permute-start.8 = (f32[256,128]{1,0:T(8,128)S(1)}, f32[256,128]{1,0:T(8,128)S(1)}, u32[]{:S(2)}, u32[]{:S(2)}) collective-permute-start(f32[256,128]{1,0:T(8,128)S(1)} %collective-permute-done.7), channel_id=1, source_target_pairs={{0,1},{1,2},{2,3},{3,4},{4,5},{5,6},{6,7},{7,8},{8,9},{9,10},{10,1... | collective-permute-start | bytes 393224 | tf_op jit(solution)/shard_map/ppermute | solution.py:23
  72.3 7.1 %collective-permute-start.9 = (f32[256,128]{1,0:T(8,128)S(1)}, f32[256,128]{1,0:T(8,128)S(1)}, u32[]{:S(2)}, u32[]{:S(2)}) collective-permute-start(f32[256,128]{1,0:T(8,128)S(1)} %collective-permute-done.8), channel_id=1, source_target_pairs={{0,1},{1,2},{2,3},{3,4},{4,5},{5,6},{6,7},{7,8},{8,9},{9,10},{10,1... | collective-permute-start | bytes 393224 | tf_op jit(solution)/shard_map/ppermute | solution.py:23
  79.4 7.1 %collective-permute-start.10 = (f32[256,128]{1,0:T(8,128)S(1)}, f32[256,128]{1,0:T(8,128)S(1)}, u32[]{:S(2)}, u32[]{:S(2)}) collective-permute-start(f32[256,128]{1,0:T(8,128)S(1)} %collective-permute-done.9), channel_id=1, source_target_pairs={{0,1},{1,2},{2,3},{3,4},{4,5},{5,6},{6,7},{7,8},{8,9},{9,10},{10,1... | collective-permute-start | bytes 393224 | tf_op jit(solution)/shard_map/ppermute | solution.py:23
  86.5 7.1 %collective-permute-start.11 = (f32[256,128]{1,0:T(8,128)S(1)}, f32[256,128]{1,0:T(8,128)S(1)}, u32[]{:S(2)}, u32[]{:S(2)}) collective-permute-start(f32[256,128]{1,0:T(8,128)S(1)} %collective-permute-done.10), channel_id=1, source_target_pairs={{0,1},{1,2},{2,3},{3,4},{4,5},{5,6},{6,7},{7,8},{8,9},{9,10},{10,1... | collective-permute-start | bytes 393224 | tf_op jit(solution)/shard_map/ppermute | solution.py:23
  93.6 7.1 %collective-permute-start.12 = (f32[256,128]{1,0:T(8,128)S(1)}, f32[256,128]{1,0:T(8,128)S(1)}, u32[]{:S(2)}, u32[]{:S(2)}) collective-permute-start(f32[256,128]{1,0:T(8,128)S(1)} %collective-permute-done.11), channel_id=1, source_target_pairs={{0,1},{1,2},{2,3},{3,4},{4,5},{5,6},{6,7},{7,8},{8,9},{9,10},{10,1... | collective-permute-start | bytes 393224 | tf_op jit(solution)/shard_map/ppermute | solution.py:23
  100.7 7.1 %collective-permute-start.13 = (f32[256,128]{1,0:T(8,128)S(1)}, f32[256,128]{1,0:T(8,128)S(1)}, u32[]{:S(2)}, u32[]{:S(2)}) collective-permute-start(f32[256,128]{1,0:T(8,128)S(1)} %collective-permute-done.12), channel_id=1, source_target_pairs={{0,1},{1,2},{2,3},{3,4},{4,5},{5,6},{6,7},{7,8},{8,9},{9,10},{10,1... | collective-permute-start | bytes 393224 | tf_op jit(solution)/shard_map/ppermute | solution.py:23
  107.7 7.1 %collective-permute-start.14 = (f32[256,128]{1,0:T(8,128)S(1)}, f32[256,128]{1,0:T(8,128)S(1)}, u32[]{:S(2)}, u32[]{:S(2)}) collective-permute-start(f32[256,128]{1,0:T(8,128)S(1)} %collective-permute-done.13), channel_id=1, source_target_pairs={{0,1},{1,2},{2,3},{3,4},{4,5},{5,6},{6,7},{7,8},{8,9},{9,10},{10,1... | collective-permute-start | bytes 393224 | tf_op jit(solution)/shard_map/ppermute | solution.py:23
  107.8 7.4 %copy-start.2 = (f32[256,128]{1,0:T(8,128)S(1)}, f32[256,128]{1,0:T(8,128)}, u32[]{:S(2)}) copy-start(f32[256,128]{1,0:T(8,128)} %param.10) | copy-start | bytes 393220
  115.5 2.0 copy-start
  120.3 11.7 %copy-start.3 = (s32[48]{0:T(128)S(1)}, s32[48]{0:T(128)}, u32[]{:S(2)}) copy-start(s32[48]{0:T(128)} %param.7) | copy-start | bytes 580
  142.3 151.1 %all-reduce.5.cloned.1.call-start = ((), (), s32[]{:S(2)}) async-start(), calls=%async_computation.1 | async-start | bytes 1048576 | tf_op jit(solution)/shard_map/psum | solution.py:55
  244.2 12.2 %copy-start.4 = (s32[48]{0:T(128)S(1)}, s32[48]{0:T(128)}, u32[]{:S(2)}) copy-start(s32[48]{0:T(128)} %param.8) | copy-start | bytes 580
  256.4 37.1 %copy-start.1 = (f32[1024,128]{1,0:T(8,128)S(1)}, f32[1024,128]{1,0:T(8,128)}, u32[]{:S(2)}) copy-start(f32[1024,128]{1,0:T(8,128)} %param.11) | copy-start | bytes 1572868
Sparse Core Ops, SparseCore 0:
  142.5 95.9 all-reduce.2
  265.5 27.9 all-reduce.4
